TPU v7x, 512 devices: a whole 4x8x8 slice. The times are simulated.
512 devices in a mesh: tm: 8 (over x, z_hi), vert: 64 (over y, z_lo, core).
Axes of the slice: x: 4, y: 8, z: 8 (z_hi: 2, z_lo: 4; z = z_hi * 4 + z_lo), core: 2. Of those that a mesh axis runs over, the one named last changes fastest.
Arguments:
- frames: bfloat16 [16, 8192, 256], P('tm', 'vert'), may hold values from -12 to 12
- cotangent: bfloat16 [16, 8192, 256], P('tm', 'vert'), may hold values from -200 to 200
- table: int32 [8192, 7], P('vert'), may hold values from -1 to 8191, as said below
- w_conv: bfloat16 [1792, 256], replicated, may hold values from -0.125 to 0.125
- w_attn: bfloat16 [4, 256, 256], replicated, may hold values from -0.375 to 0.375
Outputs:
- grad_frames: bfloat16 [16, 8192, 256], P('tm', 'vert')
- grad_conv: bfloat16 [1792, 256], replicated
- grad_attn: bfloat16 [4, 256, 256], replicated
Inputs may be any that keep to these rules, and one draw needn't show every extreme that they name: `table`: each entry of row v is -1 (an empty slot) or a vertex at most 64 places from v in the vertex order; slot 0 is v itself; some entries lie exactly 64 places away on either side.
All inputs are finite; a program needn't handle non-finite values.
Results may differ from a plain program's by a relative error of at most 0.014.
The roundings to bfloat16 on the way count: a program that leaves them out, or rounds other values in their place, can miss the bound.
Values may be sent and summed in bfloat16 or wider, within the bound.
No kernel may reach another device: no remote copies, remote signals or barrier semaphores. Data moves between devices by JAX's collectives and lax.ppermute only.
A program may use at most 64 MiB of HBM per device.

v0:
```python
import math
import jax
import jax.numpy as jnp
from jax import lax
from jax.sharding import PartitionSpec as P

TF = 16
HEADS = 8
HW = 64


def extended_2(block, sides, width):
    for axis, dim in sides:
        count = lax.axis_size(axis)
        forward = [(i, i + 1) for i in range(count - 1)]
        backward = [(target, source) for source, target in forward]
        low = lax.ppermute(
            lax.slice_in_dim(block, block.shape[dim] - width, None, axis=dim), axis, forward
        )
        high = lax.ppermute(lax.slice_in_dim(block, 0, width, axis=dim), axis, backward)
        block = jnp.concatenate([low, block, high], axis=dim)
    return block


def cross_rows(left, right):
    return lax.dot_general(
        left, right, (((0,), (0,)), ((), ())), preferred_element_type=jnp.float32
    )


def project(rows, weight):
    return jnp.dot(rows, weight, preferred_element_type=jnp.float32).astype(jnp.bfloat16)


def frame_attention(query_rows, key_rows, value_rows, grad_out):
    frames_q, verts, width = query_rows.shape
    head_dim = width // HEADS
    scaling = head_dim ** (-0.5)
    query_heads = query_rows.reshape(frames_q, verts, HEADS, head_dim)
    key_heads = key_rows.reshape(-1, verts, HEADS, head_dim)
    value_heads = value_rows.reshape(-1, verts, HEADS, head_dim)
    grad_heads = grad_out.reshape(frames_q, verts, HEADS, head_dim)
    scores = (
        jnp.einsum("frhd,grhd->rhfg", query_heads, key_heads, preferred_element_type=jnp.float32)
        * scaling
    )
    top_score = jnp.max(scores, axis=-1, keepdims=True)
    expo = jnp.exp(scores - top_score)
    probs = expo / jnp.sum(expo, axis=-1, keepdims=True)
    probs_b = probs.astype(jnp.bfloat16)
    attended = jnp.einsum(
        "rhfg,grhd->frhd", probs_b, value_heads, preferred_element_type=jnp.float32
    ).astype(jnp.bfloat16)
    grad_value = jnp.einsum(
        "rhfg,frhd->grhd", probs_b, grad_heads, preferred_element_type=jnp.float32
    ).astype(jnp.bfloat16)
    grad_probs = jnp.einsum(
        "frhd,grhd->rhfg", grad_heads, value_heads, preferred_element_type=jnp.float32
    )
    inner_sum = jnp.sum(probs * grad_probs, axis=-1, keepdims=True)
    grad_scores = (scaling * probs * (grad_probs - inner_sum)).astype(jnp.bfloat16)
    grad_query = jnp.einsum(
        "rhfg,grhd->frhd", grad_scores, key_heads, preferred_element_type=jnp.float32
    ).astype(jnp.bfloat16)
    grad_key = jnp.einsum(
        "rhfg,frhd->grhd", grad_scores, query_heads, preferred_element_type=jnp.float32
    ).astype(jnp.bfloat16)
    return (
        attended.reshape(frames_q, verts, width),
        grad_query.reshape(frames_q, verts, width),
        grad_key.reshape(-1, verts, width),
        grad_value.reshape(-1, verts, width),
    )


def body(frames, cotangent, table, w_conv, w_attn):
    local_frames, patch, width = frames.shape
    stencil = table.shape[1]
    start = lax.axis_index("vert") * patch
    extended = extended_2(frames, (("vert", 1),), HW)
    padded = jnp.concatenate([extended, jnp.zeros((local_frames, 1, width), jnp.bfloat16)], axis=1)
    blank_row = patch + 2 * HW
    local_index = jnp.where(table < 0, blank_row, table - start + HW).reshape(-1)
    gathered = jnp.take(padded, local_index, axis=1).reshape(local_frames * patch, stencil * width)
    conv_pre = jnp.dot(gathered, w_conv, preferred_element_type=jnp.float32)
    gate_sig = jax.nn.sigmoid(conv_pre)
    hidden = (frames.reshape(-1, width).astype(jnp.float32) + conv_pre * gate_sig).astype(
        jnp.bfloat16
    )
    hidden_time, grad_time = (
        lax.all_to_all(
            hidden.reshape(local_frames, patch, width),
            "tm",
            split_axis=1,
            concat_axis=0,
            tiled=True,
        ),
        lax.all_to_all(cotangent, "tm", split_axis=1, concat_axis=0, tiled=True),
    )
    shape3 = hidden_time.shape
    rows_time = hidden_time.reshape(-1, width)
    grad_rows = grad_time.reshape(-1, width)
    query_rows = project(rows_time, w_attn[0])
    key_rows = project(rows_time, w_attn[1])
    value_rows = project(rows_time, w_attn[2])
    grad_out = project(grad_rows, w_attn[3].T)
    attended, grad_query, grad_key, grad_value = frame_attention(
        query_rows.reshape(shape3),
        key_rows.reshape(shape3),
        value_rows.reshape(shape3),
        grad_out.reshape(shape3),
    )
    grad_wout = cross_rows(attended.reshape(-1, width), grad_rows)
    grad_query = grad_query.reshape(-1, width)
    grad_key = grad_key.reshape(-1, width)
    grad_value = grad_value.reshape(-1, width)
    grad_hidden = (
        grad_rows.astype(jnp.float32)
        + jnp.dot(grad_query, w_attn[0].T, preferred_element_type=jnp.float32)
        + jnp.dot(grad_key, w_attn[1].T, preferred_element_type=jnp.float32)
        + jnp.dot(grad_value, w_attn[2].T, preferred_element_type=jnp.float32)
    ).astype(jnp.bfloat16)
    weight_parts = [
        cross_rows(rows_time, grad_query),
        cross_rows(rows_time, grad_key),
        cross_rows(rows_time, grad_value),
    ]
    back_hidden = lax.all_to_all(
        grad_hidden.reshape(shape3), "tm", split_axis=0, concat_axis=1, tiled=True
    )
    grad_attn = jnp.stack(weight_parts + [grad_wout])
    back_rows = back_hidden.reshape(-1, width)
    grad_pre = (
        back_rows.astype(jnp.float32) * gate_sig * (1.0 + conv_pre * (1.0 - gate_sig))
    ).astype(jnp.bfloat16)
    grad_conv = cross_rows(gathered, grad_pre)
    grad_gathered = lax.dot_general(
        grad_pre, w_conv, (((1,), (1,)), ((), ())), preferred_element_type=jnp.float32
    )
    grad_ext = (
        jnp.zeros((local_frames, blank_row + 1, width), jnp.float32)
        .at[:, local_index]
        .add(grad_gathered.reshape(local_frames, patch * stencil, width))
    )
    rim = jnp.concatenate([grad_ext[:, :HW], grad_ext[:, patch + HW : patch + 2 * HW]], axis=1)
    arrived = extended_2(rim, (("vert", 1),), HW)
    grad_local = grad_ext[:, HW : HW + patch]
    grad_local = grad_local.at[:, :HW].add(arrived[:, :HW])
    grad_local = grad_local.at[:, patch - HW :].add(arrived[:, 3 * HW :])
    grad_frames = (back_hidden.astype(jnp.float32) + grad_local).astype(jnp.bfloat16)
    grad_conv, grad_attn = lax.psum((grad_conv, grad_attn), ("tm", "vert"))
    scaling = 1.0 / math.sqrt(TF * patch * lax.axis_size("vert"))
    return (
        grad_frames,
        (grad_conv * scaling).astype(jnp.bfloat16),
        (grad_attn * scaling).astype(jnp.bfloat16),
    )


def solution(mesh):
    return jax.shard_map(
        body,
        mesh=mesh,
        in_specs=(P("tm", "vert", None), P("tm", "vert", None), P("vert", None), P(), P()),
        out_specs=(P("tm", "vert", None), P(), P()),
        check_vma=False,
    )
```

profile of v0, /device:TPU:24, one launch (start us, length us, event | category | flops | bytes accessed | tf_op | source)
XLA Modules:
  0.0 392.5 jit_solution(10169680832873045731)
XLA Ops:
  7.2 1.1 copy.75
  8.4 1.9 collective-permute-start
  10.3 7.2 %collective-permute-start.1 = (bf16[2,64,256]{2,0,1:T(2,128)(2,1)S(1)}, bf16[2,64,256]{2,0,1:T(2,128)(2,1)S(1)}, u32[]{:S(2)}, u32[]{:S(2)}) collective-permute-start(bf16[2,64,256]{2,0,1:T(2,128)(2,1)S(1)} %get-tuple-element.44), channel_id=1, source_target_pairs={{1,0},{2,1},{3,2},{4,3},{5,4},{6,5},{7,6},{8,7},{9,8},{10,9},{11,1... | collective-permute-start | bytes 196616 | tf_op jit(solution)/shard_map/ppermute | solution.py:20
  17.6 1.7 copy.72
  19.3 11.9 %all-to-all-start = ((bf16[2,128,256]{2,0,1:T(2,128)(2,1)}), bf16[2,128,256]{2,0,1:T(2,128)(2,1)S(1)}, u32[]{:S(2)}, u32[]{:S(2)}) async-start(bf16[2,128,256]{2,0,1:T(2,128)(2,1)} %copy.72), calls=%async_computation | async-start | bytes 262144 | tf_op jit(solution)/shard_map/all_to_all | solution.py:98
  31.1 0.7 add_select_fusion
  31.9 0.2 reshape.145
  32.1 0.2 reshape.144
  32.4 0.5 maximum_maximum_fusion
  32.9 4.5 %gather_fusion = bf16[896,2,256]{2,1,0:T(2,128)(2,1)S(1)} fusion(bf16[2,257,256]{2,0,1:T(2,128)(2,1)S(1)} %maximum_maximum_fusion, s32[1024]{0:T(1024)S(1)} %pad_clamp_fusion), kind=kCustom, calls=%fused_computation | custom fusion | bytes 1838592 | tf_op jit(solution)/shard_map/jit(_take)/gather | solution.py:84
  37.4 3.3 fusion.8
  40.9 0.9 select_n.33
  41.8 1.1 fusion.18
  42.9 0.8 copy.80
  43.7 9.6 %all-to-all-start.1 = ((bf16[2,128,256]{2,0,1:T(2,128)(2,1)}), bf16[2,128,256]{2,0,1:T(2,128)(2,1)S(1)}, u32[]{:S(2)}, u32[]{:S(2)}) async-start(bf16[2,128,256]{2,0,1:T(2,128)(2,1)} %copy.80), calls=%async_computation.1 | async-start | bytes 262144 | tf_op jit(solution)/shard_map/all_to_all | solution.py:91
  53.4 0.2 convolution_convert_fusion.5
  53.6 1.0 reshape_reshape.26
  54.6 9.3 %all-to-all-done.1 = bf16[2,128,256]{2,0,1:T(2,128)(2,1)S(1)} async-done(((bf16[2,128,256]{2,0,1:T(2,128)(2,1)}), bf16[2,128,256]{2,0,1:T(2,128)(2,1)S(1)}, u32[]{:S(2)}, u32[]{:S(2)}) %all-to-all-start.1) | async-done | bytes 131104 | tf_op jit(solution)/shard_map/all_to_all | solution.py:91
  64.0 0.2 convolution_convert_fusion.7
  64.2 0.2 convolution_convert_fusion.6
  64.4 0.2 convolution_convert_fusion.4
  64.5 0.2 reshape_reshape.24
  64.8 0.2 reshape_reshape.25
  65.0 1.0 reshape_reshape.27
  66.1 2.0 fusion.53
  68.1 2.5 multiply_reduce_fusion
  70.5 0.3 multiply_convert_fusion.2
  70.9 1.3 fusion.5
  72.2 0.5 fusion.3
  72.7 1.3 fusion.6
  74.0 1.3 fusion.4
  75.3 0.1 copy.89
  75.5 0.4 reshape_reshape.28
  75.8 0.9 convolution_bitcast_fusion.3
  76.7 1.8 convolution_add_fusion.2
  78.6 0.1 copy.91
  78.7 0.4 reshape_reshape.29
  79.1 0.9 convolution_bitcast_fusion.2
  80.0 1.2 copy.93
  81.3 0.4 reshape_reshape.30
  81.6 0.9 convolution_bitcast_fusion.1
  82.5 1.2 copy.99
  83.7 0.4 reshape_reshape.31
  84.1 1.2 convolution_add_fusion.1
  85.3 0.9 fusion.7
  86.2 3.4 all-to-all-start.2
  89.6 0.2 convolution_bitcast_fusion
  89.9 2.1 pad_maximum_fusion
  92.0 8.1 %all-to-all-done.2 = bf16[16,16,256]{2,1,0:T(8,128)(2,1)S(1)} async-done(((bf16[16,16,256]{2,1,0:T(8,128)(2,1)}), bf16[16,16,256]{2,1,0:T(8,128)(2,1)S(1)}, u32[]{:S(2)}, u32[]{:S(2)}) %all-to-all-start.2) | async-done | bytes 131104 | tf_op jit(solution)/shard_map/all_to_all | solution.py:128
  100.3 1.7 fusion.59
  102.0 1.7 fusion.58
  103.7 1.6 reshape.164
  105.3 2.7 copy.136
  108.1 62.6 %scatter_fusion = f32[2,257,256]{2,0,1:T(2,128)S(1)} fusion(f32[2,257,256]{2,0,1:T(2,128)S(1)} %broadcast_in_dim.28, s32[896]{0:T(1024)S(1)} %fusion.40, f32[896,2,256]{2,1,0:T(2,128)} %bitcast.98), kind=kCustom, calls=%fused_computation.1 | custom fusion | flops 458752 | bytes 5508608 | tf_op jit(solution)/shard_map/scatter-add | solution.py:143
  170.8 1.9 collective-permute-start.2
  172.7 0.2 copy.94
  172.9 6.3 %collective-permute-start.3 = (f32[2,64,256]{2,0,1:T(2,128)S(1)}, f32[2,64,256]{2,0,1:T(2,128)S(1)}, u32[]{:S(2)}, u32[]{:S(2)}) collective-permute-start(f32[2,64,256]{2,0,1:T(2,128)S(1)} %get-tuple-element.41), channel_id=1, source_target_pairs={{1,0},{2,1},{3,2},{4,3},{5,4},{6,5},{7,6},{8,7},{9,8},{10,9},{11,1... | collective-permute-start | bytes 393224 | tf_op jit(solution)/shard_map/ppermute | solution.py:20
  179.3 0.6 collective-permute-done.2
  180.0 1.8 collective-permute-done.3
  181.9 0.2 fusion.21
  182.1 0.7 copy.100
  182.8 199.3 %all-reduce.3.cloned.1.call-done = (f32[1792,256]{1,0:T(8,128)}, f32[4,256,256]{2,1,0:T(8,128)}) async-done(((f32[1792,256]{1,0:T(8,128)}, f32[4,256,256]{2,1,0:T(8,128)}), (f32[1792,256]{1,0:T(8,128)}, f32[4,256,256]{2,1,0:T(8,128)})) %all-reduce.3.cloned.1.call-update) | async-done | bytes 2883600 | tf_op jit(solution)/shard_map/psum | solution.py:151
  382.1 2.7 multiply_convert_fusion
  384.8 0.9 multiply_convert_fusion.1
  (45 shorter events, 1.0 us)
Async XLA Ops:
  7.2 34.6 %copy-start = (bf16[1792,256]{1,0:T(8,128)(2,1)S(1)}, bf16[1792,256]{1,0:T(8,128)(2,1)}, u32[]{:S(2)}) copy-start(bf16[1792,256]{1,0:T(8,128)(2,1)} %param.12) | copy-start | bytes 2752516
  8.4 24.0 %collective-permute-start = (bf16[2,64,256]{2,0,1:T(2,128)(2,1)S(1)}, bf16[2,64,256]{2,0,1:T(2,128)(2,1)S(1)}, u32[]{:S(2)}, u32[]{:S(2)}) collective-permute-start(bf16[2,64,256]{2,0,1:T(2,128)(2,1)S(1)} %get-tuple-element.43), channel_id=1, source_target_pairs={{0,1},{1,2},{2,3},{3,4},{4,5},{5,6},{6,7},{7,8},{8,9},{9,10},{10,1... | collective-permute-start | bytes 196616 | tf_op jit(solution)/shard_map/ppermute | solution.py:17
  10.3 22.1 %collective-permute-start.1 = (bf16[2,64,256]{2,0,1:T(2,128)(2,1)S(1)}, bf16[2,64,256]{2,0,1:T(2,128)(2,1)S(1)}, u32[]{:S(2)}, u32[]{:S(2)}) collective-permute-start(bf16[2,64,256]{2,0,1:T(2,128)(2,1)S(1)} %get-tuple-element.44), channel_id=1, source_target_pairs={{1,0},{2,1},{3,2},{4,3},{5,4},{6,5},{7,6},{8,7},{9,8},{10,9},{11,1... | collective-permute-start | bytes 196616 | tf_op jit(solution)/shard_map/ppermute | solution.py:20
  19.3 24.5 %all-to-all-start = ((bf16[2,128,256]{2,0,1:T(2,128)(2,1)}), bf16[2,128,256]{2,0,1:T(2,128)(2,1)S(1)}, u32[]{:S(2)}, u32[]{:S(2)}) async-start(bf16[2,128,256]{2,0,1:T(2,128)(2,1)} %copy.72), calls=%async_computation | async-start | bytes 262144 | tf_op jit(solution)/shard_map/all_to_all | solution.py:98
  40.7 1.0 copy-start.10
  41.8 11.6 %copy-start.2 = (bf16[4,256,256]{2,1,0:T(8,128)(2,1)S(1)}, bf16[4,256,256]{2,1,0:T(8,128)(2,1)}, u32[]{:S(2)}) copy-start(bf16[4,256,256]{2,1,0:T(8,128)(2,1)} %param.13) | copy-start | bytes 1572868
  43.7 20.2 %all-to-all-start.1 = ((bf16[2,128,256]{2,0,1:T(2,128)(2,1)}), bf16[2,128,256]{2,0,1:T(2,128)(2,1)S(1)}, u32[]{:S(2)}, u32[]{:S(2)}) async-start(bf16[2,128,256]{2,0,1:T(2,128)(2,1)} %copy.80), calls=%async_computation.1 | async-start | bytes 262144 | tf_op jit(solution)/shard_map/all_to_all | solution.py:91
  68.0 2.5 copy-start.5
  70.9 1.8 copy-start.7
  72.6 1.4 copy-start.8
  75.3 3.3 copy-start.1
  80.0 4.1 %copy-start.3 = (bf16[4,256,256]{2,1,0:T(8,128)(2,1)S(1)}, bf16[4,256,256]{2,1,0:T(8,128)(2,1)}, u32[]{:S(2)}) copy-start(bf16[4,256,256]{2,1,0:T(8,128)(2,1)} %param.13) | copy-start | bytes 1572868
  84.1 5.8 %copy-start.6 = (f32[1,256,256]{2,1,0:T(8,128)S(1)}, f32[1,256,256]{2,1,0:T(8,128)}, u32[]{:S(2)}) copy-start(f32[1,256,256]{2,1,0:T(8,128)} %convolution_bitcast_fusion.1) | copy-start | bytes 786436
  86.2 13.9 %all-to-all-start.2 = ((bf16[16,16,256]{2,1,0:T(8,128)(2,1)}), bf16[16,16,256]{2,1,0:T(8,128)(2,1)S(1)}, u32[]{:S(2)}, u32[]{:S(2)}) async-start(bf16[16,16,256]{2,1,0:T(8,128)(2,1)} %bitcast.17), calls=%async_computation.2 | async-start | bytes 262144 | tf_op jit(solution)/shard_map/all_to_all | solution.py:128
  89.6 10.6 %copy-start.9 = (f32[256,256]{1,0:T(8,128)S(1)}, f32[256,256]{1,0:T(8,128)}, u32[]{:S(2)}) copy-start(f32[256,256]{1,0:T(8,128)} %get-tuple-element.46) | copy-start | bytes 786436
  89.6 292.5 %all-reduce.3.cloned.1.call-start = ((), (), s32[]{:S(2)}) async-start(), calls=%async_computation.3 | async-start | bytes 5767168 | tf_op jit(solution)/shard_map/psum | solution.py:151
  170.8 9.2 %collective-permute-start.2 = (f32[2,64,256]{2,0,1:T(2,128)S(1)}, f32[2,64,256]{2,0,1:T(2,128)S(1)}, u32[]{:S(2)}, u32[]{:S(2)}) collective-permute-start(f32[2,64,256]{2,0,1:T(2,128)S(1)} %get-tuple-element.42), channel_id=1, source_target_pairs={{0,1},{1,2},{2,3},{3,4},{4,5},{5,6},{6,7},{7,8},{8,9},{9,10},{10,1... | collective-permute-start | bytes 393224 | tf_op jit(solution)/shard_map/ppermute | solution.py:17
  172.9 8.8 %collective-permute-start.3 = (f32[2,64,256]{2,0,1:T(2,128)S(1)}, f32[2,64,256]{2,0,1:T(2,128)S(1)}, u32[]{:S(2)}, u32[]{:S(2)}) collective-permute-start(f32[2,64,256]{2,0,1:T(2,128)S(1)} %get-tuple-element.41), channel_id=1, source_target_pairs={{1,0},{2,1},{3,2},{4,3},{5,4},{6,5},{7,6},{8,7},{9,8},{10,9},{11,1... | collective-permute-start | bytes 393224 | tf_op jit(solution)/shard_map/ppermute | solution.py:20
  382.1 2.7 copy-start.4
Sparse Core Ops, SparseCore 0:
  102.1 279.8 all-reduce.2
where the time goes:
time: 397 us; the launch traced here: 393 us
  waiting for transfers between devices  219 us (55%)
  other arithmetic  73.7 us (19%)
  starting transfers between devices  42.3 us (11%)
  local copies, waits for them, and re-layouts  21.8 us (5%)
  matrix products  21.1 us (5%)
  between operations  14.5 us (4%)
    psum x1, waiting for transfers between devices, body(): grad_conv, grad_attn = lax.psum((grad_conv, grad_attn), ('tm', 'vert'))  199 us
    scatter-add x1, other arithmetic, body(): grad_ext = jnp.zeros((local_frames, blank_row + 1, width), jnp.float32).a...  62.6 us
    ppermute x2, starting transfers between devices, extended_2(): lax.ppermute(lax.slice_in_dim(block, 0, width, axis=dim), axis, backward)  13.6 us
    all_to_all x1, starting transfers between devices, body(): lax.all_to_all(cotangent, 'tm', split_axis=1, concat_axis=0, tiled=True)  11.9 us
    all_to_all x1, starting transfers between devices, body(): lax.all_to_all(hidden.reshape(local_frames, patch, width), 'tm', split_ax...  9.61 us
    all_to_all x1, waiting for transfers between devices, body(): lax.all_to_all(hidden.reshape(local_frames, patch, width), 'tm', split_ax...  9.32 us
    all_to_all x1, waiting for transfers between devices, body(): lax.all_to_all(grad_hidden.reshape(shape3), 'tm', split_axis=0, concat_ax...  8.14 us
  transfers between devices with their start and end apart: 8, of which 5 were waited for; matrix products, arithmetic and copies ran while one was open for 22% of the time, Pallas kernels for 0%

commit v1 on v0

--- a/solution.py
+++ b/solution.py
@@ -148,7 +148,7 @@
     grad_local = grad_local.at[:, :HW].add(arrived[:, :HW])
     grad_local = grad_local.at[:, patch - HW :].add(arrived[:, 3 * HW :])
     grad_frames = (back_hidden.astype(jnp.float32) + grad_local).astype(jnp.bfloat16)
-    grad_conv, grad_attn = lax.psum((grad_conv, grad_attn), ("tm", "vert"))
+    grad_conv, grad_attn = lax.psum(lax.psum((grad_conv, grad_attn), "vert"), "tm")
     scaling = 1.0 / math.sqrt(TF * patch * lax.axis_size("vert"))
     return (
         grad_frames,

time: 397 us -> 925 us (2.33)
  the two profiles are of different devices: /device:TPU:24 before, /device:TPU:1 now
where the time goes in v1:
time: 925 us; the launch traced here: 920 us
  waiting for transfers between devices  751 us (81%)
  other arithmetic  73.6 us (8%)
  starting transfers between devices  38.2 us (4%)
  local copies, waits for them, and re-layouts  21.8 us (2%)
  matrix products  21.1 us (2%)
  between operations  14.5 us (2%)
    psum x1, waiting for transfers between devices, body(): lax.psum((grad_conv, grad_attn), 'vert')  546 us
    psum x1, waiting for transfers between devices, body(): lax.psum(lax.psum((grad_conv, grad_attn), 'vert'), 'tm')  182 us
    scatter-add x1, other arithmetic, body(): grad_ext = jnp.zeros((local_frames, blank_row + 1, width), jnp.float32).a...  62.6 us
  transfers between devices with their start and end apart: 9, of which 6 were waited for; matrix products, arithmetic and copies ran while one was open for 10% of the time, Pallas kernels for 0%

profile of v1, /device:TPU:1, one launch (start us, length us, event | category | flops | bytes accessed | tf_op | source)
XLA Modules:
  0.0 920.0 jit_solution(1976495826019323786)
XLA Ops:
  7.2 1.1 copy.75
  8.4 5.4 collective-permute-start
  13.8 4.7 collective-permute-start.1
  18.5 1.7 copy.72
  20.2 8.8 all-to-all-start
  29.0 0.7 add_select_fusion
  29.8 0.2 reshape.145
  30.0 0.2 reshape.144
  30.3 0.5 maximum_maximum_fusion
  30.7 4.5 gather_fusion
  35.3 3.3 fusion.8
  38.7 0.9 select_n.33
  39.6 1.1 fusion.18
  40.8 0.8 copy.80
  41.6 9.1 all-to-all-start.1
  50.7 0.2 convolution_convert_fusion.5
  50.9 1.0 reshape_reshape.26
  51.9 8.3 all-to-all-done.1
  60.3 0.2 convolution_convert_fusion.7
  60.5 0.2 convolution_convert_fusion.6
  60.7 0.2 convolution_convert_fusion.4
  60.9 0.2 reshape_reshape.24
  61.1 0.2 reshape_reshape.25
  61.4 1.0 reshape_reshape.27
  62.4 2.0 fusion.53
  64.4 2.5 multiply_reduce_fusion
  66.8 0.3 multiply_convert_fusion.2
  67.2 1.3 fusion.5
  68.5 0.5 fusion.3
  69.0 1.3 fusion.6
  70.3 1.3 fusion.4
  71.6 0.1 copy.89
  71.8 0.4 reshape_reshape.28
  72.1 0.9 convolution_bitcast_fusion.3
  73.1 1.8 convolution_add_fusion.2
  75.0 0.4 reshape_reshape.29
  75.4 0.9 convolution_bitcast_fusion.2
  76.3 1.2 copy.93
  77.6 0.4 reshape_reshape.30
  77.9 0.9 convolution_bitcast_fusion.1
  78.9 1.2 copy.99
  80.0 0.4 reshape_reshape.31
  80.4 1.2 convolution_add_fusion.1
  81.6 0.9 fusion.7
  82.5 3.4 all-to-all-start.2
  86.0 0.2 convolution_bitcast_fusion
  86.2 2.1 pad_maximum_fusion
  88.3 7.5 all-to-all-done.2
  95.9 1.7 fusion.59
  97.7 546.0 %all-reduce.5.cloned.1.call-done = (f32[1792,256]{1,0:T(8,128)}, f32[4,256,256]{2,1,0:T(8,128)}) async-done(((f32[1792,256]{1,0:T(8,128)}, f32[4,256,256]{2,1,0:T(8,128)}), (f32[1792,256]{1,0:T(8,128)}, f32[4,256,256]{2,1,0:T(8,128)})) %all-reduce.5.cloned.1.call-update) | async-done | bytes 2883600 | tf_op jit(solution)/shard_map/psum | solution.py:151
  643.8 1.7 fusion.58
  645.5 1.6 reshape.164
  647.0 2.7 copy.136
  649.9 62.6 %scatter_fusion = f32[2,257,256]{2,0,1:T(2,128)S(1)} fusion(f32[2,257,256]{2,0,1:T(2,128)S(1)} %broadcast_in_dim.28, s32[896]{0:T(1024)S(1)} %fusion.40, f32[896,2,256]{2,1,0:T(2,128)} %bitcast.98), kind=kCustom, calls=%fused_computation.1 | custom fusion | flops 458752 | bytes 5508608 | tf_op jit(solution)/shard_map/scatter-add | solution.py:143
  712.5 3.3 collective-permute-start.2
  715.8 0.2 copy.94
  716.0 3.6 collective-permute-start.3
  719.6 1.4 collective-permute-done.2
  721.1 5.5 collective-permute-done.3
  726.7 0.2 fusion.21
  726.9 0.7 copy.100
  727.6 182.0 %all-reduce.7.cloned.1.call-done = (f32[1792,256]{1,0:T(8,128)}, f32[4,256,256]{2,1,0:T(8,128)}) async-done(((f32[1792,256]{1,0:T(8,128)}, f32[4,256,256]{2,1,0:T(8,128)}), (f32[1792,256]{1,0:T(8,128)}, f32[4,256,256]{2,1,0:T(8,128)})) %all-reduce.7.cloned.1.call-update) | async-done | bytes 2883600 | tf_op jit(solution)/shard_map/psum | solution.py:151
  909.6 2.7 multiply_convert_fusion
  912.3 0.9 multiply_convert_fusion.1
  (48 shorter events, 1.2 us)
Async XLA Ops:
  7.2 32.5 %copy-start = (bf16[1792,256]{1,0:T(8,128)(2,1)S(1)}, bf16[1792,256]{1,0:T(8,128)(2,1)}, u32[]{:S(2)}) copy-start(bf16[1792,256]{1,0:T(8,128)(2,1)} %param.12) | copy-start | bytes 2752516
  8.4 21.9 %collective-permute-start = (bf16[2,64,256]{2,0,1:T(2,128)(2,1)S(1)}, bf16[2,64,256]{2,0,1:T(2,128)(2,1)S(1)}, u32[]{:S(2)}, u32[]{:S(2)}) collective-permute-start(bf16[2,64,256]{2,0,1:T(2,128)(2,1)S(1)} %get-tuple-element.45), channel_id=1, source_target_pairs={{0,1},{1,2},{2,3},{3,4},{4,5},{5,6},{6,7},{7,8},{8,9},{9,10},{10,1... | collective-permute-start | bytes 196616 | tf_op jit(solution)/shard_map/ppermute | solution.py:17
  13.8 16.5 %collective-permute-start.1 = (bf16[2,64,256]{2,0,1:T(2,128)(2,1)S(1)}, bf16[2,64,256]{2,0,1:T(2,128)(2,1)S(1)}, u32[]{:S(2)}, u32[]{:S(2)}) collective-permute-start(bf16[2,64,256]{2,0,1:T(2,128)(2,1)S(1)} %get-tuple-element.46), channel_id=1, source_target_pairs={{1,0},{2,1},{3,2},{4,3},{5,4},{6,5},{7,6},{8,7},{9,8},{10,9},{11,1... | collective-permute-start | bytes 196616 | tf_op jit(solution)/shard_map/ppermute | solution.py:20
  20.2 21.4 %all-to-all-start = ((bf16[2,128,256]{2,0,1:T(2,128)(2,1)}), bf16[2,128,256]{2,0,1:T(2,128)(2,1)S(1)}, u32[]{:S(2)}, u32[]{:S(2)}) async-start(bf16[2,128,256]{2,0,1:T(2,128)(2,1)} %copy.72), calls=%async_computation | async-start | bytes 262144 | tf_op jit(solution)/shard_map/all_to_all | solution.py:98
  38.6 1.0 copy-start.10
  39.6 11.0 %copy-start.2 = (bf16[4,256,256]{2,1,0:T(8,128)(2,1)S(1)}, bf16[4,256,256]{2,1,0:T(8,128)(2,1)}, u32[]{:S(2)}) copy-start(bf16[4,256,256]{2,1,0:T(8,128)(2,1)} %param.13) | copy-start | bytes 1572868
  41.6 18.7 %all-to-all-start.1 = ((bf16[2,128,256]{2,0,1:T(2,128)(2,1)}), bf16[2,128,256]{2,0,1:T(2,128)(2,1)S(1)}, u32[]{:S(2)}, u32[]{:S(2)}) async-start(bf16[2,128,256]{2,0,1:T(2,128)(2,1)} %copy.80), calls=%async_computation.1 | async-start | bytes 262144 | tf_op jit(solution)/shard_map/all_to_all | solution.py:91
  64.4 2.5 copy-start.5
  67.2 1.8 copy-start.7
  69.0 1.4 copy-start.8
  71.6 3.3 copy-start.1
  76.3 4.1 copy-start.3
  80.4 5.8 copy-start.6
  82.5 13.2 %all-to-all-start.2 = ((bf16[16,16,256]{2,1,0:T(8,128)(2,1)}), bf16[16,16,256]{2,1,0:T(8,128)(2,1)S(1)}, u32[]{:S(2)}, u32[]{:S(2)}) async-start(bf16[16,16,256]{2,1,0:T(8,128)(2,1)} %bitcast.17), calls=%async_computation.2 | async-start | bytes 262144 | tf_op jit(solution)/shard_map/all_to_all | solution.py:128
  85.9 9.9 %copy-start.9 = (f32[256,256]{1,0:T(8,128)S(1)}, f32[256,256]{1,0:T(8,128)}, u32[]{:S(2)}) copy-start(f32[256,256]{1,0:T(8,128)} %get-tuple-element.48) | copy-start | bytes 786436
  85.9 557.8 %all-reduce.5.cloned.1.call-start = ((), (), s32[]{:S(2)}) async-start(), calls=%async_computation.3 | async-start | bytes 5767168 | tf_op jit(solution)/shard_map/psum | solution.py:151
  97.7 811.9 %all-reduce.7.cloned.1.call-start = ((), (), s32[]{:S(2)}) async-start(), calls=%async_computation.4 | async-start | bytes 5767168 | tf_op jit(solution)/shard_map/psum | solution.py:151
  712.5 8.5 collective-permute-start.2
  716.0 10.6 %collective-permute-start.3 = (f32[2,64,256]{2,0,1:T(2,128)S(1)}, f32[2,64,256]{2,0,1:T(2,128)S(1)}, u32[]{:S(2)}, u32[]{:S(2)}) collective-permute-start(f32[2,64,256]{2,0,1:T(2,128)S(1)} %get-tuple-element.43), channel_id=1, source_target_pairs={{1,0},{2,1},{3,2},{4,3},{5,4},{6,5},{7,6},{8,7},{9,8},{10,9},{11,1... | collective-permute-start | bytes 393224 | tf_op jit(solution)/shard_map/ppermute | solution.py:20
  909.6 2.7 copy-start.4
Sparse Core Ops, SparseCore 0:
  97.8 545.9 all-reduce.4
  646.8 262.7 all-reduce.6
